TPU v7x, 32 devices: a whole 2x2x4 slice. The times are simulated.
32 devices in a mesh: groups: 2 (over y), seq: 4 (over z), head: 2 (over x), tile: 2 (over core).
Axes of the slice: x: 2, y: 2, z: 4, core: 2. Of those that a mesh axis runs over, the one named last changes fastest.
Arguments:
- query_states: bfloat16 [4608, 3072], P(('groups', 'seq', 'tile'), 'head'), parts along dimension 0, may hold values from -5 to 5
- key_states: bfloat16 [4608, 3072], P(('groups', 'seq', 'tile'), 'head'), parts along dimension 0, may hold values from -5 to 5
- value_states: bfloat16 [4608, 3072], P(('groups', 'seq', 'tile'), 'head'), parts along dimension 0, may hold values from -6 to 6
- residual: bfloat16 [4608, 3072], P(('groups', 'seq', 'tile'), 'head'), parts along dimension 0, may hold values from -6 to 6
- out_weight: bfloat16 [3072, 3072], P(None, 'head'), may hold values from -0.109375 to 0.109375
- gate_scale: float32 [6144], P(('groups', 'head')), parts along dimension 0, may hold values from 2 to 8
Outputs:
- block_out: bfloat16 [4608, 3072], P(('groups', 'seq', 'tile'), 'head'), parts along dimension 0
There are 2 independent parts, one for each index of `groups`. A program takes and returns all parts, laid end to end along the dimension named above; an argument that names none is the same for every part. Nothing has to cross between parts.
All inputs are finite; a program needn't handle non-finite values.
Results may differ from a plain program's by a relative error of at most 0.0065.
Values may be sent and summed in bfloat16 or wider, within the bound.
A program may use at most 128 MiB of HBM per device.

v0:
```python
import math
import jax
import jax.numpy as jnp
from jax import lax
from jax.sharding import PartitionSpec as P

HD = 128


def per_device(query_states, key_states, value_states, residual, out_weight, gate_scale):
    row_count = query_states.shape[0]
    heads_here = query_states.shape[1] // HD
    score_scale = 1.0 / math.sqrt(HD)
    query_heads = query_states.reshape(row_count, heads_here, HD)
    running_max = jnp.full((heads_here, row_count), -jnp.inf, jnp.float32)
    denominator = jnp.zeros((heads_here, row_count), jnp.float32)
    numerator = jnp.zeros((row_count, heads_here, HD), jnp.float32)
    key_heads = lax.all_gather(key_states, ("seq", "tile"), axis=0, tiled=True).reshape(
        -1, heads_here, HD
    )
    value_heads = lax.all_gather(value_states, ("seq", "tile"), axis=0, tiled=True).reshape(
        -1, heads_here, HD
    )
    scores = (
        jnp.einsum("qhd,khd->hqk", query_heads, key_heads, preferred_element_type=jnp.float32)
        * score_scale
    )
    new_max = jnp.max(scores, axis=2)
    shrink = jnp.exp(running_max - new_max)
    weights = jnp.exp(scores - new_max[:, :, None])
    denominator = denominator * shrink + jnp.sum(weights, axis=2)
    probs = weights.astype(jnp.bfloat16)
    numerator = numerator * shrink.T[:, :, None] + jnp.einsum(
        "hqk,khd->qhd", probs, value_heads, preferred_element_type=jnp.float32
    )
    running_max, denominator, numerator = (new_max, denominator, numerator)
    attended = (
        (numerator / denominator.T[:, :, None])
        .astype(jnp.bfloat16)
        .reshape(row_count, heads_here * HD)
    )
    projected = jnp.dot(
        lax.all_gather(attended, "head", axis=1, tiled=True),
        out_weight,
        preferred_element_type=jnp.float32,
    )
    return (residual.astype(jnp.float32) + gate_scale[None, :] * projected).astype(jnp.bfloat16)


def solution(mesh):
    placed = (
        P(("groups", "seq", "tile"), "head"),
        P(("groups", "seq", "tile"), "head"),
        P(("groups", "seq", "tile"), "head"),
        P(("groups", "seq", "tile"), "head"),
        P(None, "head"),
        P(("groups", "head")),
    )
    return jax.shard_map(
        per_device,
        mesh=mesh,
        in_specs=placed,
        out_specs=P(("groups", "seq", "tile"), "head"),
        check_vma=False,
    )
```

profile of v0, /device:TPU:0, one launch (start us, length us, event | category | flops | bytes accessed | tf_op | source)
XLA Modules:
  0.0 223.8 jit_solution(13114338873008730694)
XLA Ops:
  6.5 0.0 copy-start
  6.5 0.0 all-gather.4.cloned.1.call-start
  6.5 0.7 all-gather.4.cloned.1.call-update
  7.3 0.0 all-gather.6.cloned.1.call-start
  7.3 0.7 all-gather.6.cloned.1.call-update
  8.0 0.0 all-gather.8.cloned.1.call-start
  8.1 74.9 %all-gather.4.cloned.1.call-done = bf16[2304,1536]{1,0:T(8,128)(2,1)} async-done(((bf16[288,1536]{1,0:T(8,128)(2,1)}), bf16[2304,1536]{1,0:T(8,128)(2,1)}) %all-gather.4.cloned.1.call-update) | async-done | bytes 7077904 | tf_op jit(solution)/shard_map/all_gather | solution.py:18
  83.0 10.3 %copy.14 = bf16[2304,1536]{0,1:T(8,128)(2,1)} copy(bf16[2304,1536]{1,0:T(8,128)(2,1)} %all-gather.4.cloned.1.call-done) | data formatting | bytes 14155776 | tf_op jit(solution)/shard_map/all_gather | solution.py:18
  93.3 0.0 copy-done
  93.3 14.8 %multiply_reduce_fusion = (f32[12,288]{1,0:T(8,128)S(1)}, f32[12,288,2304]{2,1,0:T(8,128)}) fusion(bf16[2304,12,128]{0,2,1:T(8,128)(2,1)} %bitcast.34, bf16[288,1536]{1,0:T(8,128)(2,1)S(1)} %copy-done), kind=kOutput, calls=%fused_computation.1 | convolution fusion | flops 2054353536 | bytes 39826944 | tf_op jit(solution)/shard_map/qhd,khd->hqk/dot_general | solution.py:25
  108.2 14.0 %fusion = f32[12,288]{1,0:T(8,128)S(1)} fusion(f32[12,288,2304]{2,1,0:T(8,128)} %get-tuple-element.6, f32[12,288]{1,0:T(8,128)S(1)} %get-tuple-element.5), kind=kLoop, calls=%fused_computation.2 | loop fusion | flops 23884416 | bytes 31878144 | tf_op jit(solution)/shard_map/reduce_sum | solution.py:31
  122.2 32.4 %all-gather.6.cloned.1.call-done = bf16[2304,1536]{1,0:T(8,128)(2,1)} async-done(((bf16[288,1536]{1,0:T(8,128)(2,1)}), bf16[2304,1536]{1,0:T(8,128)(2,1)}) %all-gather.6.cloned.1.call-update) | async-done | bytes 7077904 | tf_op jit(solution)/shard_map/all_gather | solution.py:21
  154.5 10.3 %copy.17 = bf16[2304,1536]{0,1:T(8,128)(2,1)} copy(bf16[2304,1536]{1,0:T(8,128)(2,1)} %all-gather.6.cloned.1.call-done) | data formatting | bytes 14155776 | tf_op jit(solution)/shard_map/all_gather | solution.py:21
  164.8 0.0 copy-start.2
  164.8 0.0 copy-start.3
  164.8 15.1 %fusion.12 = bf16[12,36,8,128]{3,2,1,0:T(8,128)(2,1)S(1)} fusion(bf16[2304,12,128]{0,2,1:T(8,128)(2,1)} %bitcast.35, f32[12,288,2304]{2,1,0:T(8,128)} %get-tuple-element.6, f32[12,288]{1,0:T(8,128)S(1)} %get-tuple-element.5, f32[288,12]{0,1:T(8,128)S(1)} %bitcast_add_fusion.1, f32[288,12]{0,1:T(8,128)S(1)} %multiply_bitcast_fusion), kind=kOutput, calls=%fused_computation.13 | convolution fusion | flops 2063646720 | bytes 39854592 | tf_op jit(solution)/shard_map/hqk,khd->qhd/dot_general | solution.py:33
  179.9 1.1 copy.31
  181.0 0.0 all-gather.8.cloned.1.call-update
  181.0 28.2 %all-gather.8.cloned.1.call-done = bf16[288,3072]{1,0:T(8,128)(2,1)} async-done(((bf16[288,1536]{1,0:T(8,128)(2,1)}), bf16[288,3072]{1,0:T(8,128)(2,1)}) %all-gather.8.cloned.1.call-update) | async-done | bytes 1769488 | tf_op jit(solution)/shard_map/all_gather | solution.py:43
  209.2 0.0 copy-done.2
  209.2 0.0 copy-done.3
  209.2 0.0 copy-start.1
  209.2 8.1 %fusion.7 = bf16[288,1536]{1,0:T(8,128)(2,1)} fusion(bf16[288,3072]{1,0:T(8,128)(2,1)} %all-gather.8.cloned.1.call-done, bf16[3072,1536]{1,0:T(8,128)(2,1)} %param.10, bf16[288,1536]{1,0:T(8,128)(2,1)S(1)} %copy-done.2, f32[1536]{0:T(1024)S(1)} %copy-done.3), kind=kOutput, calls=%fused_computation.9 | convolution fusion | flops 2719678464 | bytes 12982272 | tf_op jit(solution)/shard_map/dot_general | solution.py:42
  217.3 0.0 copy-done.1
  (2 shorter events, 0.0 us)
Async XLA Ops:
  6.5 86.8 %copy-start = (bf16[288,1536]{1,0:T(8,128)(2,1)S(1)}, bf16[288,1536]{1,0:T(8,128)(2,1)}, u32[]{:S(2)}) copy-start(bf16[288,1536]{1,0:T(8,128)(2,1)} %param.6) | copy-start | bytes 2654212
  6.5 76.5 %all-gather.4.cloned.1.call-start = ((), (), s32[]{:S(2)}) async-start(), calls=%async_computation | async-start | bytes 7962624 | tf_op jit(solution)/shard_map/all_gather | solution.py:18
  7.3 147.3 %all-gather.6.cloned.1.call-start = ((), (), s32[]{:S(2)}) async-start(), calls=%async_computation.1 | async-start | bytes 7962624 | tf_op jit(solution)/shard_map/all_gather | solution.py:21
  8.0 201.2 %all-gather.8.cloned.1.call-start = ((), (), s32[]{:S(2)}) async-start(), calls=%async_computation.2 | async-start | bytes 2654208 | tf_op jit(solution)/shard_map/all_gather | solution.py:43
  164.8 44.4 %copy-start.2 = (bf16[288,1536]{1,0:T(8,128)(2,1)S(1)}, bf16[288,1536]{1,0:T(8,128)(2,1)}, u32[]{:S(2)}) copy-start(bf16[288,1536]{1,0:T(8,128)(2,1)} %param.9) | copy-start | bytes 2654212
  164.8 44.4 %copy-start.3 = (f32[1536]{0:T(1024)S(1)}, f32[1536]{0:T(1024)}, u32[]{:S(2)}) copy-start(f32[1536]{0:T(1024)} %param.11) | copy-start | bytes 18436
  209.2 8.1 %copy-start.1 = (bf16[288,1536]{1,0:T(8,128)(2,1)S(1)}, bf16[288,1536]{1,0:T(8,128)(2,1)}, u32[]{:S(2)}) copy-start(bf16[288,1536]{1,0:T(8,128)(2,1)} %param.6) | copy-start | bytes 2654212
Sparse Core Ops, SparseCore 0:
  9.0 73.9 all-gather.3
  84.6 69.8 all-gather.5
  181.1 28.0 all-gather.7
where the time goes:
time: 225 us; the launch traced here: 224 us
  waiting for transfers between devices  137 us (61%)
  matrix products  38 us (17%)
  local copies, waits for them, and re-layouts  21.7 us (10%)
  other arithmetic  14 us (6%)
  between operations  13.1 us (6%)
    all_gather x1, waiting for transfers between devices, per_device(): lax.all_gather(key_states, ('seq', 'tile'), axis=0, tiled=True)  74.9 us
    all_gather x1, waiting for transfers between devices, per_device(): lax.all_gather(value_states, ('seq', 'tile'), axis=0, tiled=True)  32.4 us
    all_gather x1, waiting for transfers between devices, per_device(): lax.all_gather(attended, 'head', axis=1, tiled=True)  28.2 us
    dot_general x1, matrix products, per_device(): jnp.einsum('hqk,khd->qhd', probs, value_heads, preferred_element_type=jnp...  15.1 us
    dot_general x1, matrix products, per_device(): jnp.einsum('qhd,khd->hqk', query_heads, key_heads, preferred_element_type...  14.8 us
    reduce_sum x1, other arithmetic, per_device(): denominator = denominator * shrink + jnp.sum(weights, axis=2)  14 us
    all_gather x1, local copies, waits for them, and re-layouts, per_device(): lax.all_gather(key_states, ('seq', 'tile'), axis=0, tiled=True)  10.3 us
    all_gather x1, local copies, waits for them, and re-layouts, per_device(): lax.all_gather(value_states, ('seq', 'tile'), axis=0, tiled=True)  10.3 us
  transfers between devices with their start and end apart: 3, of which 3 were waited for; matrix products, arithmetic and copies ran while one was open for 17% of the time, Pallas kernels for 0%

commit v1 on v0

--- a/solution.py
+++ b/solution.py
@@ -5,6 +5,29 @@
 from jax.sharding import PartitionSpec as P
 
 HD = 128
+
+
+def derive_the_links(body):
+    field_out, mixed_arr, z2 = (
+        lax.axis_size(("seq", "tile")),
+        lax.axis_index(("seq", "tile")),
+        body.shape[0],
+    )
+    gallery = [(t, (t + 1) % field_out) for t in range(field_out)]
+    fields = [(t, (t - 1) % field_out) for t in range(field_out)]
+    v1 = jnp.zeros((*body.shape[:0], field_out * z2, *body.shape[1:]), body.dtype)
+    v1 = lax.dynamic_update_slice_in_dim(v1, body, mixed_arr * z2, axis=0)
+    x_new = then = body
+    s_next = field_out // 2
+    for pp in tuple(range(1, s_next + 1)):
+        x_new = lax.ppermute(x_new, ("seq", "tile"), gallery)
+        v1 = lax.dynamic_update_slice_in_dim(v1, x_new, (mixed_arr - pp) % field_out * z2, axis=0)
+        if pp < field_out - s_next:
+            then = lax.ppermute(then, ("seq", "tile"), fields)
+            v1 = lax.dynamic_update_slice_in_dim(
+                v1, then, (mixed_arr + pp) % field_out * z2, axis=0
+            )
+    return v1
 
 
 def per_device(query_states, key_states, value_states, residual, out_weight, gate_scale):
@@ -15,9 +38,7 @@
     running_max = jnp.full((heads_here, row_count), -jnp.inf, jnp.float32)
     denominator = jnp.zeros((heads_here, row_count), jnp.float32)
     numerator = jnp.zeros((row_count, heads_here, HD), jnp.float32)
-    key_heads = lax.all_gather(key_states, ("seq", "tile"), axis=0, tiled=True).reshape(
-        -1, heads_here, HD
-    )
+    key_heads = derive_the_links(key_states).reshape(-1, heads_here, HD)
     value_heads = lax.all_gather(value_states, ("seq", "tile"), axis=0, tiled=True).reshape(
         -1, heads_here, HD
     )

time: 225 us -> 345 us (1.53)
  local copies, waits for them, and re-layouts: 21.7 us -> 124 us
  starting transfers between devices: 0.08 us -> 21.5 us
  waiting for transfers between devices: 137 us -> 131 us
    dynamic_update_slice x0 -> x8, local copies, waits for them, and re-layouts: none -> 97.3 us  [the longest x4 48.2 us: derive_the_links(): lax.dynamic_update_slice_in_dim(v1, x_new, (mixed_arr - pp) % field_out *...]
    ppermute x0 -> x7, waiting for transfers between devices: none -> 88.8 us  [the longest x4 71.2 us: derive_the_links(): x_new = lax.ppermute(x_new, ('seq', 'tile'), gallery)]
    all_gather x1 -> x0, waiting for transfers between devices: 74.9 us -> none  [per_device(): lax.all_gather(key_states, ('seq', 'tile'), axis=0, tiled=True)]
    all_gather x1, waiting for transfers between devices: 32.4 us -> 0.02 us  [per_device(): lax.all_gather(value_states, ('seq', 'tile'), axis=0, tiled=True)]
    ppermute x0 -> x7, starting transfers between devices: none -> 21.5 us  [the longest x3 11.6 us: derive_the_links(): then = lax.ppermute(then, ('seq', 'tile'), fields)]
    all_gather x1, waiting for transfers between devices: 28.2 us -> 41.2 us  [per_device(): lax.all_gather(attended, 'head', axis=1, tiled=True)]
    ppermute x0 -> x7, local copies, waits for them, and re-layouts: none -> 10.6 us  [the longest x4 5.65 us: derive_the_links(): x_new = lax.ppermute(x_new, ('seq', 'tile'), gallery)]
    all_gather x1 -> x0, local copies, waits for them, and re-layouts: 10.3 us -> none  [per_device(): lax.all_gather(key_states, ('seq', 'tile'), axis=0, tiled=True)]
  transfers between devices with their start and end apart: 3 -> 9, of which waited for: 3 -> 6; matrix products, arithmetic and copies ran while one was open for 17% -> 41% of each run, Pallas kernels for 0% -> 0%
where the time goes in v1:
time: 345 us; the launch traced here: 342 us
  waiting for transfers between devices  131 us (38%)
  local copies, waits for them, and re-layouts  124 us (36%)
  matrix products  37.8 us (11%)
  starting transfers between devices  21.5 us (6%)
  other arithmetic  13.9 us (4%)
  between operations  13.6 us (4%)
    ppermute x4, waiting for transfers between devices, derive_the_links(): x_new = lax.ppermute(x_new, ('seq', 'tile'), gallery)  71.2 us
    dynamic_update_slice x4, local copies, waits for them, and re-layouts, derive_the_links(): lax.dynamic_update_slice_in_dim(v1, x_new, (mixed_arr - pp) % field_out *...  48.2 us
    all_gather x1, waiting for transfers between devices, per_device(): lax.all_gather(attended, 'head', axis=1, tiled=True)  41.2 us
    dynamic_update_slice x3, local copies, waits for them, and re-layouts, derive_the_links(): lax.dynamic_update_slice_in_dim(v1, then, (mixed_arr + pp) % field_out *...  37.8 us
    ppermute x3, waiting for transfers between devices, derive_the_links(): then = lax.ppermute(then, ('seq', 'tile'), fields)  17.6 us
    dot_general x1, matrix products, per_device(): jnp.einsum('hqk,khd->qhd', probs, value_heads, preferred_element_type=jnp...  15.1 us
    dot_general x1, matrix products, per_device(): jnp.einsum('qhd,khd->hqk', query_heads, key_heads, preferred_element_type...  14.6 us
    reduce_sum x1, other arithmetic, per_device(): denominator = denominator * shrink + jnp.sum(weights, axis=2)  13.8 us
  transfers between devices with their start and end apart: 9, of which 6 were waited for; matrix products, arithmetic and copies ran while one was open for 41% of the time, Pallas kernels for 0%

profile of v1, /device:TPU:0, one launch (start us, length us, event | category | flops | bytes accessed | tf_op | source)
XLA Modules:
  0.0 341.5 jit_solution(5106186980798070295)
XLA Ops:
  7.8 4.1 %collective-permute-start.1 = (bf16[288,1536]{1,0:T(8,128)(2,1)}, bf16[288,1536]{1,0:T(8,128)(2,1)S(1)}, u32[]{:S(2)}, u32[]{:S(2)}) collective-permute-start(bf16[288,1536]{1,0:T(8,128)(2,1)} %param.7), channel_id=1, source_target_pairs={{0,13},{1,0},{4,1},{5,4},{8,5},{9,8},{12,9},{13,12},{2,15},{3,2},{... | collective-permute-start | bytes 2654216 | tf_op jit(solution)/shard_map/ppermute | solution.py:26
  11.9 22.8 %collective-permute-done = bf16[288,1536]{1,0:T(8,128)(2,1)S(1)} collective-permute-done((bf16[288,1536]{1,0:T(8,128)(2,1)}, bf16[288,1536]{1,0:T(8,128)(2,1)S(1)}, u32[]{:S(2)}, u32[]{:S(2)}) %collective-permute-start) | collective-permute-done | bytes 884768 | tf_op jit(solution)/shard_map/ppermute | solution.py:23
  35.5 7.6 %collective-permute-done.1 = bf16[288,1536]{1,0:T(8,128)(2,1)S(1)} collective-permute-done((bf16[288,1536]{1,0:T(8,128)(2,1)}, bf16[288,1536]{1,0:T(8,128)(2,1)S(1)}, u32[]{:S(2)}, u32[]{:S(2)}) %collective-permute-start.1) | collective-permute-done | bytes 884768 | tf_op jit(solution)/shard_map/ppermute | solution.py:26
  43.1 3.6 %collective-permute-start.3 = (bf16[288,1536]{1,0:T(8,128)(2,1)S(1)}, bf16[288,1536]{1,0:T(8,128)(2,1)}, u32[]{:S(2)}, u32[]{:S(2)}) collective-permute-start(bf16[288,1536]{1,0:T(8,128)(2,1)S(1)} %collective-permute-done.1), channel_id=1, source_target_pairs={{0,13},{1,0},{4,1},{5,4},{8,5},{9,8},{12,9},{13,12},{2,15},{3,2},{... | collective-permute-start | bytes 2654216 | tf_op jit(solution)/shard_map/ppermute | solution.py:26
  46.7 26.9 %collective-permute-done.2 = bf16[288,1536]{1,0:T(8,128)(2,1)S(1)} collective-permute-done((bf16[288,1536]{1,0:T(8,128)(2,1)S(1)}, bf16[288,1536]{1,0:T(8,128)(2,1)S(1)}, u32[]{:S(2)}, u32[]{:S(2)}) %collective-permute-start.2) | collective-permute-done | bytes 884768 | tf_op jit(solution)/shard_map/ppermute | solution.py:23
  74.7 10.0 %collective-permute-done.3 = bf16[288,1536]{1,0:T(8,128)(2,1)} collective-permute-done((bf16[288,1536]{1,0:T(8,128)(2,1)S(1)}, bf16[288,1536]{1,0:T(8,128)(2,1)}, u32[]{:S(2)}, u32[]{:S(2)}) %collective-permute-start.3) | collective-permute-done | bytes 884768 | tf_op jit(solution)/shard_map/ppermute | solution.py:26
  84.7 3.8 %collective-permute-start.5 = (bf16[288,1536]{1,0:T(8,128)(2,1)}, bf16[288,1536]{1,0:T(8,128)(2,1)}, u32[]{:S(2)}, u32[]{:S(2)}) collective-permute-start(bf16[288,1536]{1,0:T(8,128)(2,1)} %collective-permute-done.3), channel_id=1, source_target_pairs={{0,13},{1,0},{4,1},{5,4},{8,5},{9,8},{12,9},{13,12},{2,15},{3,2},{... | collective-permute-start | bytes 2654216 | tf_op jit(solution)/shard_map/ppermute | solution.py:26
  88.5 21.5 %collective-permute-done.4 = bf16[288,1536]{1,0:T(8,128)(2,1)S(1)} collective-permute-done((bf16[288,1536]{1,0:T(8,128)(2,1)S(1)}, bf16[288,1536]{1,0:T(8,128)(2,1)S(1)}, u32[]{:S(2)}, u32[]{:S(2)}) %collective-permute-start.4) | collective-permute-done | bytes 884768 | tf_op jit(solution)/shard_map/ppermute | solution.py:23
  110.0 7.5 %collective-permute-start.6 = (bf16[288,1536]{1,0:T(8,128)(2,1)S(1)}, bf16[288,1536]{1,0:T(8,128)(2,1)}, u32[]{:S(2)}, u32[]{:S(2)}) collective-permute-start(bf16[288,1536]{1,0:T(8,128)(2,1)S(1)} %collective-permute-done.4), channel_id=1, source_target_pairs={{0,1},{1,4},{4,5},{5,8},{8,9},{9,12},{12,13},{13,0},{2,3},{3,6},{6... | collective-permute-start | bytes 2654216 | tf_op jit(solution)/shard_map/ppermute | solution.py:23
  117.6 1.6 copy.16
  119.3 3.3 broadcast_in_dim.7
  122.5 11.3 %dynamic_update_slice.24 = bf16[2304,1536]{0,1:T(8,128)(2,1)} dynamic-update-slice(bf16[2304,1536]{0,1:T(8,128)(2,1)} %broadcast_in_dim.7, bf16[288,1536]{0,1:T(8,128)(2,1)S(1)} %copy.16, s32[]{:T(128)S(6)} %select_n.55, s32[]{:T(128)} %constant.65.clone.1) | dynamic-update-slice | bytes 1769476 | tf_op jit(solution)/shard_map/dynamic_update_slice | solution.py:19
  133.8 1.6 copy.17
  135.5 11.8 %dynamic_update_slice.25 = bf16[2304,1536]{0,1:T(8,128)(2,1)} dynamic-update-slice(bf16[2304,1536]{0,1:T(8,128)(2,1)} %dynamic_update_slice.24, bf16[288,1536]{0,1:T(8,128)(2,1)S(1)} %copy.17, s32[]{:T(128)S(6)} %select_n.57, s32[]{:T(128)} %constant.65.clone.1) | dynamic-update-slice | bytes 1769476 | tf_op jit(solution)/shard_map/dynamic_update_slice | solution.py:24
  147.3 1.6 copy.18
  149.0 12.6 %dynamic_update_slice.26 = bf16[2304,1536]{0,1:T(8,128)(2,1)} dynamic-update-slice(bf16[2304,1536]{0,1:T(8,128)(2,1)} %dynamic_update_slice.25, bf16[288,1536]{0,1:T(8,128)(2,1)S(1)} %copy.18, s32[]{:T(128)S(6)} %select_n.59, s32[]{:T(128)} %constant.65.clone.1) | dynamic-update-slice | bytes 1769476 | tf_op jit(solution)/shard_map/dynamic_update_slice | solution.py:27
  161.6 1.6 copy.19
  163.2 12.4 %dynamic_update_slice.27 = bf16[2304,1536]{0,1:T(8,128)(2,1)} dynamic-update-slice(bf16[2304,1536]{0,1:T(8,128)(2,1)} %dynamic_update_slice.26, bf16[288,1536]{0,1:T(8,128)(2,1)S(1)} %copy.19, s32[]{:T(128)S(6)} %select_n.61, s32[]{:T(128)} %constant.65.clone.1) | dynamic-update-slice | bytes 1769476 | tf_op jit(solution)/shard_map/dynamic_update_slice | solution.py:24
  175.7 1.6 copy.20
  177.3 12.6 %dynamic_update_slice.28 = bf16[2304,1536]{0,1:T(8,128)(2,1)} dynamic-update-slice(bf16[2304,1536]{0,1:T(8,128)(2,1)} %dynamic_update_slice.27, bf16[288,1536]{0,1:T(8,128)(2,1)S(1)} %copy.20, s32[]{:T(128)S(6)} %select_n.63, s32[]{:T(128)} %constant.65.clone.1) | dynamic-update-slice | bytes 1769476 | tf_op jit(solution)/shard_map/dynamic_update_slice | solution.py:27
  190.6 12.6 %dynamic_update_slice.29 = bf16[2304,1536]{0,1:T(8,128)(2,1)} dynamic-update-slice(bf16[2304,1536]{0,1:T(8,128)(2,1)} %dynamic_update_slice.28, bf16[288,1536]{0,1:T(8,128)(2,1)S(1)} %copy.21, s32[]{:T(128)S(6)} %select_n.65, s32[]{:T(128)} %constant.65.clone.1) | dynamic-update-slice | bytes 1769476 | tf_op jit(solution)/shard_map/dynamic_update_slice | solution.py:24
  203.2 1.6 copy.22
  204.9 12.6 %dynamic_update_slice.30 = bf16[2304,1536]{0,1:T(8,128)(2,1)} dynamic-update-slice(bf16[2304,1536]{0,1:T(8,128)(2,1)} %dynamic_update_slice.29, bf16[288,1536]{0,1:T(8,128)(2,1)S(1)} %copy.22, s32[]{:T(128)S(6)} %select_n.67, s32[]{:T(128)} %constant.65.clone.1) | dynamic-update-slice | bytes 1769476 | tf_op jit(solution)/shard_map/dynamic_update_slice | solution.py:27
  217.5 1.6 copy.23
  219.1 11.3 %dynamic_update_slice.31 = bf16[2304,1536]{0,1:T(8,128)(2,1)} dynamic-update-slice(bf16[2304,1536]{0,1:T(8,128)(2,1)} %dynamic_update_slice.30, bf16[288,1536]{0,1:T(8,128)(2,1)S(1)} %copy.23, s32[]{:T(128)S(6)} %select_n.69, s32[]{:T(128)} %constant.65.clone.1) | dynamic-update-slice | bytes 1769476 | tf_op jit(solution)/shard_map/dynamic_update_slice | solution.py:24
  230.5 14.6 %bitcast_reduce_fusion = (f32[12,288]{1,0:T(8,128)S(1)}, f32[12,2304,288]{1,2,0:T(8,128)}) fusion(bf16[2304,12,128]{0,2,1:T(8,128)(2,1)} %bitcast.48, bf16[288,1536]{1,0:T(8,128)(2,1)S(1)} %copy-done), kind=kOutput, calls=%fused_computation.1 | convolution fusion | flops 2054353536 | bytes 39826944 | tf_op jit(solution)/shard_map/qhd,khd->hqk/dot_general | solution.py:46
  245.0 13.8 %fusion.1 = f32[12,288]{1,0:T(8,128)S(1)} fusion(f32[12,2304,288]{1,2,0:T(8,128)} %get-tuple-element.6, f32[12,288]{1,0:T(8,128)S(1)} %get-tuple-element.5), kind=kLoop, calls=%fused_computation.3 | loop fusion | flops 23884416 | bytes 31878144 | tf_op jit(solution)/shard_map/reduce_sum | solution.py:52
  258.9 10.2 %copy.26 = bf16[2304,1536]{0,1:T(8,128)(2,1)} copy(bf16[2304,1536]{1,0:T(8,128)(2,1)} %all-gather.3.cloned.1.call-done) | data formatting | bytes 14155776 | tf_op jit(solution)/shard_map/all_gather | solution.py:42
  269.2 15.1 %fusion.13 = bf16[12,36,8,128]{3,2,1,0:T(8,128)(2,1)S(1)} fusion(bf16[2304,12,128]{0,2,1:T(8,128)(2,1)} %bitcast.49, f32[12,2304,288]{1,2,0:T(8,128)} %get-tuple-element.6, f32[12,288]{1,0:T(8,128)S(1)} %get-tuple-element.5, f32[288,12]{0,1:T(8,128)S(1)} %bitcast_add_fusion.1, f32[288,12]{0,1:T(8,128)S(1)} %multiply_bitcast_fusion), kind=kOutput, calls=%fused_computation.14 | convolution fusion | flops 2063646720 | bytes 39854592 | tf_op jit(solution)/shard_map/hqk,khd->qhd/dot_general | solution.py:54
  284.3 1.1 copy.40
  285.4 41.2 %all-gather.5.cloned.1.call-done = bf16[288,3072]{1,0:T(8,128)(2,1)} async-done(((bf16[288,1536]{1,0:T(8,128)(2,1)}), bf16[288,3072]{1,0:T(8,128)(2,1)}) %all-gather.5.cloned.1.call-update) | async-done | bytes 1769488 | tf_op jit(solution)/shard_map/all_gather | solution.py:64
  326.6 8.1 %fusion.8 = bf16[288,1536]{1,0:T(8,128)(2,1)} fusion(bf16[288,3072]{1,0:T(8,128)(2,1)} %all-gather.5.cloned.1.call-done, bf16[3072,1536]{1,0:T(8,128)(2,1)} %param.10, bf16[288,1536]{1,0:T(8,128)(2,1)S(1)} %copy-done.5, f32[1536]{0:T(1024)S(1)} %copy-done.6), kind=kOutput, calls=%fused_computation.10 | convolution fusion | flops 2719678464 | bytes 12982272 | tf_op jit(solution)/shard_map/dot_general | solution.py:63
  (27 shorter events, 3.9 us)
Async XLA Ops:
  6.5 223.9 %copy-start = (bf16[288,1536]{1,0:T(8,128)(2,1)S(1)}, bf16[288,1536]{1,0:T(8,128)(2,1)}, u32[]{:S(2)}) copy-start(bf16[288,1536]{1,0:T(8,128)(2,1)} %param.6) | copy-start | bytes 2654212
  6.5 252.4 %all-gather.3.cloned.1.call-start = ((), (), s32[]{:S(2)}) async-start(), calls=%async_computation | async-start | bytes 7962624 | tf_op jit(solution)/shard_map/all_gather | solution.py:42
  7.3 319.3 %all-gather.5.cloned.1.call-start = ((), (), s32[]{:S(2)}) async-start(), calls=%async_computation.1 | async-start | bytes 2654208 | tf_op jit(solution)/shard_map/all_gather | solution.py:64
  7.3 27.4 %collective-permute-start = (bf16[288,1536]{1,0:T(8,128)(2,1)}, bf16[288,1536]{1,0:T(8,128)(2,1)S(1)}, u32[]{:S(2)}, u32[]{:S(2)}) collective-permute-start(bf16[288,1536]{1,0:T(8,128)(2,1)} %param.7), channel_id=1, source_target_pairs={{0,1},{1,4},{4,5},{5,8},{8,9},{9,12},{12,13},{13,0},{2,3},{3,6},{6... | collective-permute-start | bytes 2654216 | tf_op jit(solution)/shard_map/ppermute | solution.py:23
  7.8 35.3 %collective-permute-start.1 = (bf16[288,1536]{1,0:T(8,128)(2,1)}, bf16[288,1536]{1,0:T(8,128)(2,1)S(1)}, u32[]{:S(2)}, u32[]{:S(2)}) collective-permute-start(bf16[288,1536]{1,0:T(8,128)(2,1)} %param.7), channel_id=1, source_target_pairs={{0,13},{1,0},{4,1},{5,4},{8,5},{9,8},{12,9},{13,12},{2,15},{3,2},{... | collective-permute-start | bytes 2654216 | tf_op jit(solution)/shard_map/ppermute | solution.py:26
  34.7 82.9 %copy-start.4 = (bf16[288,1536]{1,0:T(8,128)(2,1)}, bf16[288,1536]{1,0:T(8,128)(2,1)S(1)}, u32[]{:S(2)}) copy-start(bf16[288,1536]{1,0:T(8,128)(2,1)S(1)} %collective-permute-done) | copy-start | bytes 2654212
  34.7 38.9 %collective-permute-start.2 = (bf16[288,1536]{1,0:T(8,128)(2,1)S(1)}, bf16[288,1536]{1,0:T(8,128)(2,1)S(1)}, u32[]{:S(2)}, u32[]{:S(2)}) collective-permute-start(bf16[288,1536]{1,0:T(8,128)(2,1)S(1)} %collective-permute-done), channel_id=1, source_target_pairs={{0,1},{1,4},{4,5},{5,8},{8,9},{9,12},{12,13},{13,0},{2,3},{3,6},{6... | collective-permute-start | bytes 2654216 | tf_op jit(solution)/shard_map/ppermute | solution.py:23
  43.1 66.9 %copy-start.2 = (bf16[288,1536]{1,0:T(8,128)(2,1)}, bf16[288,1536]{1,0:T(8,128)(2,1)S(1)}, u32[]{:S(2)}) copy-start(bf16[288,1536]{1,0:T(8,128)(2,1)S(1)} %collective-permute-done.1) | copy-start | bytes 2654212
  43.1 41.6 %collective-permute-start.3 = (bf16[288,1536]{1,0:T(8,128)(2,1)S(1)}, bf16[288,1536]{1,0:T(8,128)(2,1)}, u32[]{:S(2)}, u32[]{:S(2)}) collective-permute-start(bf16[288,1536]{1,0:T(8,128)(2,1)S(1)} %collective-permute-done.1), channel_id=1, source_target_pairs={{0,13},{1,0},{4,1},{5,4},{8,5},{9,8},{12,9},{13,12},{2,15},{3,2},{... | collective-permute-start | bytes 2654216 | tf_op jit(solution)/shard_map/ppermute | solution.py:26
  73.6 44.0 %copy-start.3 = (bf16[288,1536]{1,0:T(8,128)(2,1)}, bf16[288,1536]{1,0:T(8,128)(2,1)S(1)}, u32[]{:S(2)}) copy-start(bf16[288,1536]{1,0:T(8,128)(2,1)S(1)} %collective-permute-done.2) | copy-start | bytes 2654212
  73.6 36.4 %collective-permute-start.4 = (bf16[288,1536]{1,0:T(8,128)(2,1)S(1)}, bf16[288,1536]{1,0:T(8,128)(2,1)S(1)}, u32[]{:S(2)}, u32[]{:S(2)}) collective-permute-start(bf16[288,1536]{1,0:T(8,128)(2,1)S(1)} %collective-permute-done.2), channel_id=1, source_target_pairs={{0,1},{1,4},{4,5},{5,8},{8,9},{9,12},{12,13},{13,0},{2,3},{3,6},{6... | collective-permute-start | bytes 2654216 | tf_op jit(solution)/shard_map/ppermute | solution.py:23
  84.7 118.5 %collective-permute-start.5 = (bf16[288,1536]{1,0:T(8,128)(2,1)}, bf16[288,1536]{1,0:T(8,128)(2,1)}, u32[]{:S(2)}, u32[]{:S(2)}) collective-permute-start(bf16[288,1536]{1,0:T(8,128)(2,1)} %collective-permute-done.3), channel_id=1, source_target_pairs={{0,13},{1,0},{4,1},{5,4},{8,5},{9,8},{12,9},{13,12},{2,15},{3,2},{... | collective-permute-start | bytes 2654216 | tf_op jit(solution)/shard_map/ppermute | solution.py:26
  110.0 107.4 %collective-permute-start.6 = (bf16[288,1536]{1,0:T(8,128)(2,1)S(1)}, bf16[288,1536]{1,0:T(8,128)(2,1)}, u32[]{:S(2)}, u32[]{:S(2)}) collective-permute-start(bf16[288,1536]{1,0:T(8,128)(2,1)S(1)} %collective-permute-done.4), channel_id=1, source_target_pairs={{0,1},{1,4},{4,5},{5,8},{8,9},{9,12},{12,13},{13,0},{2,3},{3,6},{6... | collective-permute-start | bytes 2654216 | tf_op jit(solution)/shard_map/ppermute | solution.py:23
  269.2 57.4 %copy-start.5 = (bf16[288,1536]{1,0:T(8,128)(2,1)S(1)}, bf16[288,1536]{1,0:T(8,128)(2,1)}, u32[]{:S(2)}) copy-start(bf16[288,1536]{1,0:T(8,128)(2,1)} %param.9) | copy-start | bytes 2654212
  269.2 57.4 %copy-start.6 = (f32[1536]{0:T(1024)S(1)}, f32[1536]{0:T(1024)}, u32[]{:S(2)}) copy-start(f32[1536]{0:T(1024)} %param.11) | copy-start | bytes 18436
  326.6 8.1 %copy-start.1 = (bf16[288,1536]{1,0:T(8,128)(2,1)S(1)}, bf16[288,1536]{1,0:T(8,128)(2,1)}, u32[]{:S(2)}) copy-start(bf16[288,1536]{1,0:T(8,128)(2,1)} %param.6) | copy-start | bytes 2654212
Sparse Core Ops, SparseCore 0:
  9.0 117.7 all-gather.2
  285.5 41.0 all-gather.4
